TPU v7x, 32 devices: a whole 2x2x4 slice. The times are simulated.
32 devices in a mesh: groups: 2 (over x), agent: 8 (over z, y), tm: 2 (over core).
Axes of the slice: x: 2, y: 2, z: 4, core: 2. Of those that a mesh axis runs over, the one named last changes fastest.
Arguments:
- embedded: bfloat16 [64, 1024, 512], P(('groups', 'tm'), 'agent'), parts along dimension 0, may hold values from -6 to 6
- block_lists: int32 [16, 32, 2], P(('groups', 'agent'), 'tm'), parts along dimension 0, may hold values from 0 to 7, all different within a row; in each aligned block of 16 rows (0 to 15, 16 to 31, ..., all dimensions but the last counted through in order) at most 8 rows name the same one
- done_flags: int32 [64, 1024], P(('groups', 'tm'), 'agent'), parts along dimension 0, may hold values 0 or 1
- rewards: float32 [64, 1024], P(('groups', 'tm'), 'agent'), parts along dimension 0, may hold values from -1.2 to 1.2
- bootstrap: float32 [2048], P(('groups', 'agent')), parts along dimension 0, may hold values from -6 to 6
- agent_proj: bfloat16 [512, 1536], replicated, may hold values from -2 to 2
- agent_merge: bfloat16 [512, 512], replicated, may hold values from -0.75 to 0.75
- time_proj: bfloat16 [512, 1536], replicated, may hold values from -2 to 2
- time_merge: bfloat16 [512, 512], replicated, may hold values from -0.75 to 0.75
- value_weight: float32 [512], replicated, may hold values from -0.25 to 0.25
Outputs:
- values: float32 [64, 1024], P(('groups', 'tm'), 'agent'), parts along dimension 0
- advantages: float32 [64, 1024], P(('groups', 'tm'), 'agent'), parts along dimension 0
There are 2 independent parts, one for each index of `groups`. A program takes and returns all parts, laid end to end along the dimension named above; an argument that names none is the same for every part. Nothing has to cross between parts.
Inputs may be any that keep to these rules, and one draw needn't show every extreme that they name: `block_lists`: each row names 2 different agent blocks. Within the 16 rows of one block along the second dimension no agent block is named more than 8 times, and some agent block is named exactly 8 times.
All inputs are finite; a program needn't handle non-finite values. No bound on the sum of `done_flags` on one device may be relied on, other than what follows from the above.
Results may differ from a plain program's by a relative error of at most 0.0085.
Values may be sent and summed in bfloat16 or wider, within the bound.
A program may use at most 128 MiB of HBM per device.

v0:
```python
import math

import jax
import jax.numpy as jnp
from jax import lax
from jax.sharding import PartitionSpec as P

HEADS = 8
WINDOW = 16


discount = 0.9997
trace_decay = 0.995
epsilon = 1e-06


def from_behind(value, axis, by):
    devices = lax.axis_size(axis)
    pairs = [(i, i + by) for i in range(devices) if 0 <= i + by < devices]
    return lax.ppermute(value, axis, pairs)


def entering(value, axis, join, neutral):
    count, mine = (lax.axis_size(axis), lax.axis_index(axis))
    pieces = jax.tree.map(lambda part: lax.all_gather(part, axis), value)
    pieces = jax.tree.map(lambda part: part[::-1], pieces)
    mine = count - 1 - mine
    running = jax.tree.map(
        lambda part, zero: jnp.full_like(part, 0) + jnp.asarray(zero, part.dtype), value, neutral
    )

    def hop(position, running):
        longer = join(running, jax.tree.map(lambda part: part[position], pieces))
        return jax.tree.map(lambda new, old: jnp.where(position < mine, new, old), longer, running)

    return lax.fori_loop(0, count - 1, hop, running)


def rms_norm(values):
    return values * lax.rsqrt(jnp.mean(values * values, axis=-1, keepdims=True) + epsilon)


def softmax_rows(scores):
    shifted = scores - jnp.max(scores, axis=-1, keepdims=True)
    exponent = jnp.exp(shifted)
    return exponent / jnp.sum(exponent, axis=-1, keepdims=True)


def suffix_pass(changes, factors, inject):
    agents_here = changes.shape[1]

    def backward(running, inputs):
        change, factor, injected = inputs
        advance = change + factor * running[0]
        through = factor * running[1]
        from_value = injected + factor * running[2]
        return ((advance, through, from_value), (advance, through, from_value))

    start_state = (
        jnp.zeros((agents_here,), jnp.float32),
        jnp.ones((agents_here,), jnp.float32),
        jnp.zeros((agents_here,), jnp.float32),
    )
    final_state, outputs = lax.scan(backward, start_state, (changes, factors, inject), reverse=True)
    return outputs


def compose_split(earlier, later):
    return (later[0] + later[1] * earlier[0], later[1] * earlier[1])


def body(
    embedded,
    block_lists,
    done_flags,
    rewards,
    bootstrap,
    agent_proj,
    agent_merge,
    time_proj,
    time_merge,
    value_weight,
):
    steps_here, agents_here, model_width = embedded.shape
    list_length = block_lists.shape[2]
    head_size = model_width // HEADS
    window = WINDOW
    score_scale = head_size ** (-0.5)
    tokens = steps_here * agents_here
    blocks_count = lax.axis_size("agent")
    capacity = max(2, (2 * steps_here * list_length + blocks_count - 1) // blocks_count)
    residual = embedded.astype(jnp.float32).reshape(tokens, model_width)
    normed = rms_norm(residual).astype(jnp.bfloat16)
    projected = jnp.dot(normed, agent_proj, preferred_element_type=jnp.float32).astype(jnp.bfloat16)
    projected = projected.reshape(steps_here, agents_here, 3 * model_width)
    queries = projected[:, :, :model_width]
    keyvals = projected[:, :, model_width:]
    listed_peers = block_lists[0].reshape(-1)
    row_count = listed_peers.shape[0]
    row_steps = jnp.arange(row_count, dtype=jnp.int32) // list_length
    peer_hits = (
        listed_peers[:, None] == jnp.arange(blocks_count, dtype=jnp.int32)[None, :]
    ).astype(jnp.int32)
    earlier = jnp.cumsum(peer_hits, axis=0) - peer_hits
    slot_index = jnp.sum(earlier * peer_hits, axis=1)
    slot_hits = (slot_index[:, None] == jnp.arange(capacity, dtype=jnp.int32)[None, :]).astype(
        jnp.int32
    )
    requests = (
        jnp.einsum(
            "rp,rc->pc",
            peer_hits * (row_steps[:, None] + 1),
            slot_hits,
            preferred_element_type=jnp.int32,
        )
        - 1
    )
    wanted = lax.all_to_all(requests, "agent", split_axis=0, concat_axis=0, tiled=True)
    chosen = jnp.maximum(wanted, 0).reshape(-1)
    positions = listed_peers * capacity + slot_index
    outgoing = normed.reshape(steps_here, agents_here, model_width)[chosen]
    outgoing = outgoing.reshape(blocks_count, capacity, agents_here, model_width)
    arrived = lax.all_to_all(outgoing, "agent", split_axis=0, concat_axis=0, tiled=True)
    listed_rows = arrived.reshape(blocks_count * capacity, agents_here, model_width)[positions]
    listed = jnp.dot(
        listed_rows.reshape(-1, model_width),
        agent_proj[:, model_width:],
        preferred_element_type=jnp.float32,
    ).astype(jnp.bfloat16)
    listed = listed.reshape(steps_here, list_length * agents_here, 2 * model_width)
    step_group = math.gcd(steps_here, max(1, 512 // agents_here))
    group_count = steps_here // step_group
    all_keys = jnp.concatenate([keyvals, listed], axis=1).reshape(
        group_count, step_group, -1, 2, HEADS, head_size
    )
    query_heads = queries.reshape(group_count, step_group, agents_here, HEADS, head_size)

    def agent_group(inputs):
        query_part, key_part = inputs
        scores = (
            jnp.einsum(
                "tqhe,tkhe->thqk", query_part, key_part[:, :, 0], preferred_element_type=jnp.float32
            )
            * score_scale
        )
        attention = softmax_rows(scores).astype(jnp.bfloat16)
        return jnp.einsum(
            "thqk,tkhe->tqhe", attention, key_part[:, :, 1], preferred_element_type=jnp.float32
        ).astype(jnp.bfloat16)

    attended = lax.map(agent_group, (query_heads, all_keys))
    residual = residual + jnp.dot(
        attended.reshape(tokens, model_width), agent_merge, preferred_element_type=jnp.float32
    )
    normed = rms_norm(residual).astype(jnp.bfloat16)
    projected = jnp.dot(normed, time_proj, preferred_element_type=jnp.float32).astype(jnp.bfloat16)
    projected = projected.reshape(steps_here, agents_here, 3 * model_width)
    time_keys = projected[:, :, model_width:]
    rim_keys = from_behind(time_keys, "tm", 1)
    padded = jnp.concatenate([rim_keys, time_keys], axis=0)
    block_count = steps_here // window
    previous = padded[:steps_here].reshape(block_count, window, agents_here, 2, HEADS, head_size)
    current = padded[window:].reshape(block_count, window, agents_here, 2, HEADS, head_size)
    key_blocks = jnp.concatenate([previous, current], axis=1)
    query_blocks = projected[:, :, :model_width].reshape(
        block_count, window, agents_here, HEADS, head_size
    )
    offset = lax.axis_index("tm") * steps_here
    block_starts = offset + jnp.arange(block_count, dtype=jnp.int32) * window
    query_step = block_starts[:, None] + jnp.arange(window, dtype=jnp.int32)[None, :]
    key_step = block_starts[:, None] - window + jnp.arange(2 * window, dtype=jnp.int32)[None, :]
    allowed = (
        (key_step[:, None, :] <= query_step[:, :, None])
        & (key_step[:, None, :] > query_step[:, :, None] - window)
        & (key_step[:, None, :] >= 0)
    )
    scores = (
        jnp.einsum(
            "bqahe,bkahe->bahqk",
            query_blocks,
            key_blocks[:, :, :, 0],
            preferred_element_type=jnp.float32,
        )
        * score_scale
    )
    scores = jnp.where(allowed[:, None, None], scores, -1e30)
    attention = softmax_rows(scores).astype(jnp.bfloat16)
    attended = jnp.einsum(
        "bahqk,bkahe->bqahe", attention, key_blocks[:, :, :, 1], preferred_element_type=jnp.float32
    ).astype(jnp.bfloat16)
    residual = residual + jnp.dot(
        attended.reshape(tokens, model_width), time_merge, preferred_element_type=jnp.float32
    )
    values = jnp.sum(rms_norm(residual) * value_weight, axis=-1).reshape(steps_here, agents_here)
    living = 1.0 - done_flags.astype(jnp.float32)
    factors = discount * trace_decay * living
    last_block = lax.axis_index("tm") == lax.axis_size("tm") - 1
    arriving = from_behind(values[0], "tm", -1)
    following_last = jnp.where(last_block, bootstrap, arriving)
    following = jnp.concatenate([values[1:], following_last[None, :]], axis=0)
    changes = rewards + discount * living * following - values
    inject = jnp.zeros((steps_here, agents_here), jnp.float32)
    local_adv, gains_adv, gains_val = suffix_pass(changes, factors, inject)
    element = (local_adv[0], gains_adv[0])
    identity = (jnp.zeros((agents_here,), jnp.float32), jnp.ones((agents_here,), jnp.float32))
    carried = entering(element, "tm", compose_split, identity)
    advantages = local_adv + gains_adv * carried[0][None, :]
    return (values, advantages)


def solution(mesh):
    placed = (
        P(("groups", "tm"), "agent", None),
        P(("groups", "agent"), "tm", None),
        P(("groups", "tm"), "agent"),
        P(("groups", "tm"), "agent"),
        P(("groups", "agent")),
        P(),
        P(),
        P(),
        P(),
        P(),
    )
    return jax.shard_map(
        body,
        mesh=mesh,
        in_specs=placed,
        out_specs=(P(("groups", "tm"), "agent"), P(("groups", "tm"), "agent")),
        check_vma=False,
    )
```

profile of v0, /device:TPU:0, one launch (start us, length us, event | category | flops | bytes accessed | tf_op | source)
XLA Modules:
  0.0 488.2 jit_solution(13060431496737885862)
XLA Ops:
  2.8 7.3 %all-to-all-start = ((s32[8,1,8]{2,1,0:T(1,128)}), s32[8,1,8]{2,1,0:T(1,128)S(1)}, u32[]{:S(2)}, u32[]{:S(2)}) async-start(s32[8,1,8]{2,1,0:T(1,128)} %bitcast.11), calls=%async_computation | async-start | bytes 8192 | tf_op jit(solution)/shard_map/all_to_all | solution.py:118
  12.2 3.4 multiply_convert_fusion.1
  16.6 7.0 %gather_fusion = bf16[64,128,512]{2,1,0:T(8,128)(2,1)} fusion(bf16[16,128,512]{2,1,0:T(8,128)(2,1)} %multiply_convert_fusion.1, s32[1024]{0:T(1024)S(1)} %pad_clamp_fusion.1), kind=kCustom, calls=%fused_computation | custom fusion | bytes 16777472 | tf_op jit(solution)/shard_map/gather | solution.py:121
  23.7 5.4 %all-to-all-start.1 = ((bf16[8,8,128,512]{3,2,1,0:T(8,128)(2,1)}), bf16[8,8,128,512]{3,2,1,0:T(8,128)(2,1)}, u32[]{:S(2)}, u32[]{:S(2)}) async-start(bf16[8,8,128,512]{3,2,1,0:T(8,128)(2,1)} %bitcast.112), calls=%async_computation.1 | async-start | bytes 16777216 | tf_op jit(solution)/shard_map/all_to_all | solution.py:123
  29.1 4.2 copy.48
  33.4 5.9 %convolution_convert_fusion.2 = bf16[2048,1536]{1,0:T(8,128)(2,1)S(1)} fusion(bf16[512,1536]{1,0:T(8,128)(2,1)S(1)} %copy-done.14, f32[2048,512]{0,1:T(8,128)} %copy.48, f32[2048]{0:T(1024)S(1)} %get-tuple-element.245), kind=kOutput, calls=%fused_computation.45 | convolution fusion | flops 3226468352 | bytes 12066816 | tf_op jit(solution)/shard_map/dot_general | solution.py:94
  39.3 2.5 slice.75
  43.5 6.4 %copy.52 = bf16[16,128,1024]{1,2,0:T(8,128)(2,1)} copy(bf16[16,128,1024]{2,1,0:T(8,128)(2,1)} %slice.75) | data formatting | bytes 8388608
  49.9 7.7 %copy.38 = bf16[4,4,128,2,8,64]{2,1,0,5,4,3:T(4,128)(2,1)} copy(bf16[4,4,128,2,8,64]{2,5,4,3,1,0:T(8,128)(2,1)} %bitcast.115) | data formatting | bytes 8388608 | tf_op jit(solution)/shard_map/concatenate | solution.py:133
  57.6 3.9 copy.39
  61.5 150.2 %all-to-all-done.1 = bf16[8,8,128,512]{3,2,1,0:T(8,128)(2,1)} async-done(((bf16[8,8,128,512]{3,2,1,0:T(8,128)(2,1)}), bf16[8,8,128,512]{3,2,1,0:T(8,128)(2,1)}, u32[]{:S(2)}, u32[]{:S(2)}) %all-to-all-start.1) | async-done | bytes 8388640 | tf_op jit(solution)/shard_map/all_to_all | solution.py:123
  211.7 6.2 %gather_fusion.1 = bf16[32,128,512]{2,1,0:T(8,128)(2,1)} fusion(bf16[64,128,512]{2,1,0:T(8,128)(2,1)} %bitcast.13, s32[1024]{0:T(1024)S(1)} %pad_clamp_fusion), kind=kCustom, calls=%fused_computation.1 | custom fusion | bytes 8388736 | tf_op jit(solution)/shard_map/gather | solution.py:124
  217.9 9.0 %convolution_convert_fusion.1 = bf16[4096,1024]{1,0:T(8,128)(2,1)} fusion(bf16[4096,512]{1,0:T(8,128)(2,1)} %bitcast.123, bf16[512,1536]{1,0:T(8,128)(2,1)S(1)} %copy-done.14), kind=kOutput, calls=%fused_computation.44 | convolution fusion | flops 4299161600 | bytes 13631488 | tf_op jit(solution)/shard_map/dot_general | solution.py:125
  226.8 11.3 %copy.37 = bf16[4096,1024]{0,1:T(8,128)(2,1)} copy(bf16[4096,1024]{1,0:T(8,128)(2,1)} %convolution_convert_fusion.1) | data formatting | bytes 16777216 | tf_op jit(solution)/shard_map/convert_element_type | solution.py:129
  238.1 14.6 %concatenate.15 = bf16[4,4,256,2,8,64]{2,1,0,5,4,3:T(4,128)(2,1)} reshape(bf16[4096,1024]{0,1:T(8,128)(2,1)} %copy.37) | data formatting | bytes 16777216 | tf_op jit(solution)/shard_map/concatenate | solution.py:133
  252.7 9.5 %pad_maximum_fusion = bf16[4,4,384,2,8,64]{2,1,0,5,4,3:T(4,128)(2,1)} fusion(bf16[4,4,256,2,8,64]{2,1,0,5,4,3:T(4,128)(2,1)} %concatenate.15, bf16[4,4,128,2,8,64]{2,1,0,5,4,3:T(4,128)(2,1)} %copy.38), kind=kLoop, calls=%fused_computation.32 | loop fusion | flops 25165824 | bytes 25165824 | tf_op jit(solution)/shard_map/concatenate | solution.py:133
  262.2 104.0 %while.36 = (s32[]{:T(128)}, bf16[4,4,128,8,64]{2,1,0,4,3:T(4,128)(2,1)}, bf16[4,4,384,2,8,64]{2,1,0,5,4,3:T(4,128)(2,1)}, bf16[4,4,128,8,64]{2,4,3,1,0:T(8,128)(2,1)}, s32[]{:T(128)}) while((s32[]{:T(128)}, bf16[4,4,128,8,64]{2,1,0,4,3:T(4,128)(2,1)}, bf16[4,4,384,2,8,64]{2,1,0,5,4,3:T(4,128)(2,1)}, bf16[4,4,128,8,64]{2,4,3,1,0:T(8,128)(2,1)}, ...), condition=%wide.region_6.7_spmd, body=%wide.region_3.6_spmd.sunk | while | flops 417075968 | bytes 80774264 | solution.py:151
  262.4 3.1 constant_dynamic-slice_fusion.3
  269.9 2.6 copy-done.2
  272.5 2.1 fusion.82
  274.6 12.5 %fusion.83 = bf16[1,4,128,8,64]{2,4,3,1,0:T(8,128)(2,1)S(1)} fusion(f32[4,8,128]{2,1,0:T(8,128)S(1)} %fusion.82, bf16[4,384,2,8,64]{1,4,3,0,2:T(8,128)(2,1)} %bitcast.111, f32[4,8,128,384]{3,2,1,0:T(8,128)} %copy-done.2), kind=kOutput, calls=%fused_computation.14.clone.1 | convolution fusion | flops 209457536 | bytes 14696448 | tf_op jit(solution)/shard_map/while/body/eval_jaxpr/thqk,tkhe->tqhe/dot_general | solution.py:147
  288.4 3.0 constant_dynamic-slice_fusion.3
  295.8 2.6 copy-done.2
  300.5 12.5 %fusion.83 = bf16[1,4,128,8,64]{2,4,3,1,0:T(8,128)(2,1)S(1)} fusion(f32[4,8,128]{2,1,0:T(8,128)S(1)} %fusion.82, bf16[4,384,2,8,64]{1,4,3,0,2:T(8,128)(2,1)} %bitcast.111, f32[4,8,128,384]{3,2,1,0:T(8,128)} %copy-done.2), kind=kOutput, calls=%fused_computation.14.clone.1 | convolution fusion | flops 209457536 | bytes 14696448 | tf_op jit(solution)/shard_map/while/body/eval_jaxpr/thqk,tkhe->tqhe/dot_general | solution.py:147
  314.3 3.0 constant_dynamic-slice_fusion.3
  321.7 2.6 copy-done.2
  324.3 2.1 fusion.82
  326.4 12.5 %fusion.83 = bf16[1,4,128,8,64]{2,4,3,1,0:T(8,128)(2,1)S(1)} fusion(f32[4,8,128]{2,1,0:T(8,128)S(1)} %fusion.82, bf16[4,384,2,8,64]{1,4,3,0,2:T(8,128)(2,1)} %bitcast.111, f32[4,8,128,384]{3,2,1,0:T(8,128)} %copy-done.2), kind=kOutput, calls=%fused_computation.14.clone.1 | convolution fusion | flops 209457536 | bytes 14696448 | tf_op jit(solution)/shard_map/while/body/eval_jaxpr/thqk,tkhe->tqhe/dot_general | solution.py:147
  340.2 3.2 constant_dynamic-slice_fusion.3
  347.8 2.6 copy-done.2
  352.5 12.5 %fusion.83 = bf16[1,4,128,8,64]{2,4,3,1,0:T(8,128)(2,1)S(1)} fusion(f32[4,8,128]{2,1,0:T(8,128)S(1)} %fusion.82, bf16[4,384,2,8,64]{1,4,3,0,2:T(8,128)(2,1)} %bitcast.111, f32[4,8,128,384]{3,2,1,0:T(8,128)} %copy-done.2), kind=kOutput, calls=%fused_computation.14.clone.1 | convolution fusion | flops 209457536 | bytes 14696448 | tf_op jit(solution)/shard_map/while/body/eval_jaxpr/thqk,tkhe->tqhe/dot_general | solution.py:147
  366.2 4.5 reshape.335
  370.8 4.2 multiply_reduce_fusion.3
  375.1 4.0 convolution_convert_fusion
  379.1 2.7 copy-done.5
  381.7 2.5 slice.78
  384.2 6.4 %copy.54 = bf16[16,128,1024]{1,2,0:T(8,128)(2,1)} copy(bf16[16,128,1024]{2,1,0:T(8,128)(2,1)} %slice.78) | data formatting | bytes 8388608
  390.6 3.2 collective-permute-start
  393.9 3.1 slice.77
  397.0 13.0 %copy.44 = bf16[1,16,128,2,8,64]{5,1,4,2,3,0:T(8,128)(2,1)} copy(bf16[1,16,128,2,8,64]{2,5,4,3,1,0:T(8,128)(2,1)} %bitcast.114) | data formatting | bytes 8388608 | tf_op jit(solution)/shard_map/reshape | solution.py:163
  410.0 3.9 copy.53
  413.9 7.5 %copy.46 = bf16[16,128,8,64]{3,0,2,1:T(8,128)(2,1)} copy(bf16[16,128,8,64]{1,3,2,0:T(8,128)(2,1)} %bitcast.118) | data formatting | bytes 4194304 | tf_op jit(solution)/shard_map/reshape.8
  421.4 13.0 %copy.43 = bf16[1,16,128,2,8,64]{5,1,4,2,3,0:T(8,128)(2,1)} copy(bf16[1,16,128,2,8,64]{2,5,4,3,1,0:T(8,128)(2,1)} %bitcast.19) | data formatting | bytes 8388608 | tf_op jit(solution)/shard_map/reshape | solution.py:162
  434.4 12.3 %fusion.26 = f32[128,8,16,32]{3,2,1,0:T(8,128)} fusion(bf16[16,128,8,64]{3,0,2,1:T(8,128)(2,1)} %copy.46, bf16[1,16,128,2,8,64]{5,1,4,2,3,0:T(8,128)(2,1)} %copy.43, bf16[1,16,128,2,8,64]{5,1,4,2,3,0:T(8,128)(2,1)} %copy.44), kind=kOutput, calls=%fused_computation.35 | convolution fusion | flops 75497472 | bytes 12582912 | tf_op jit(solution)/shard_map/bqahe,bkahe->bahqk/dot_general | solution.py:178
  446.7 11.8 %fusion.65 = (f32[128,8,16]{2,1,0:T(8,128)S(1)}, f32[128,8,16,32]{3,2,1,0:T(8,128)}) fusion(f32[128,8,16,32]{3,2,1,0:T(8,128)} %fusion.26, pred[16,32]{1,0:T(8,128)(4,1)S(1)} %and_and_fusion), kind=kOutput, calls=%fused_computation.118 | output fusion | flops 3145759 | bytes 4260352 | tf_op jit(solution)/shard_map/sub | solution.py:44
  458.5 7.3 %convert_bitcast_fusion = bf16[1,16,128,8,64]{4,1,3,2,0:T(8,128)(2,1)} fusion(bf16[1,16,128,2,8,64]{5,1,4,2,3,0:T(8,128)(2,1)} %copy.44, bf16[1,16,128,2,8,64]{5,1,4,2,3,0:T(8,128)(2,1)S(1)} %copy-done.4, f32[128,8,16,32]{3,2,1,0:T(8,128)} %get-tuple-element.250, f32[128,8,16]{2,1,0:T(8,128)S(1)} %get-tuple-element.249), kind=kOutput, calls=%fused_computation.49 | convolution fusion | flops 77594624 | bytes 12648448 | tf_op jit(solution)/shard_map/bahqk,bkahe->bqahe/dot_general | solution.py:188
  465.8 8.1 %copy.47 = bf16[1,16,128,8,64]{2,1,4,3,0:T(8,128)(2,1)} copy(bf16[1,16,128,8,64]{4,1,3,2,0:T(8,128)(2,1)} %convert_bitcast_fusion) | data formatting | bytes 4194304 | tf_op jit(solution)/shard_map/convert_element_type | solution.py:190
  473.9 4.3 multiply_reduce_fusion.2
  (144 shorter events, 44.9 us)
Async XLA Ops:
  0.6 374.4 %copy-start = (bf16[512,1536]{1,0:T(8,128)(2,1)S(1)}, bf16[512,1536]{1,0:T(8,128)(2,1)}, u32[]{:S(2)}) copy-start(bf16[512,1536]{1,0:T(8,128)(2,1)} %param.21) | copy-start | bytes 4718596
  2.8 13.7 %all-to-all-start = ((s32[8,1,8]{2,1,0:T(1,128)}), s32[8,1,8]{2,1,0:T(1,128)S(1)}, u32[]{:S(2)}, u32[]{:S(2)}) async-start(s32[8,1,8]{2,1,0:T(1,128)} %bitcast.11), calls=%async_computation | async-start | bytes 8192 | tf_op jit(solution)/shard_map/all_to_all | solution.py:118
  23.7 188.0 %all-to-all-start.1 = ((bf16[8,8,128,512]{3,2,1,0:T(8,128)(2,1)}), bf16[8,8,128,512]{3,2,1,0:T(8,128)(2,1)}, u32[]{:S(2)}, u32[]{:S(2)}) async-start(bf16[8,8,128,512]{3,2,1,0:T(8,128)(2,1)} %bitcast.112), calls=%async_computation.1 | async-start | bytes 16777216 | tf_op jit(solution)/shard_map/all_to_all | solution.py:123
  29.1 4.3 copy-start.14
  41.8 1.5 copy-start.11
  266.2 1.7 copy-start.1
  269.9 2.6 copy-start.2
  292.0 1.7 copy-start.1
  295.8 2.6 copy-start.2
  318.0 1.7 copy-start.1
  321.7 2.6 copy-start.2
  344.0 1.7 copy-start.1
  347.8 2.6 copy-start.2
  366.2 4.5 copy-start.6
  375.0 4.0 copy-start.3
  379.1 2.7 copy-start.5
  390.6 30.8 %collective-permute-start = (bf16[16,128,1024]{1,2,0:T(8,128)(2,1)}, bf16[16,128,1024]{1,2,0:T(8,128)(2,1)}, u32[]{:S(2)}, u32[]{:S(2)}) collective-permute-start(bf16[16,128,1024]{1,2,0:T(8,128)(2,1)} %copy.54), channel_id=1, source_target_pairs={{0,1},{2,3},{4,5},{6,7},{8,9},{10,11},{12,13},{14,15},{16,17},{18,... | collective-permute-start | bytes 12582920 | tf_op jit(solution)/shard_map/ppermute | solution.py:20
  446.7 11.8 %copy-start.4 = (bf16[1,16,128,2,8,64]{5,1,4,2,3,0:T(8,128)(2,1)S(1)}, bf16[1,16,128,2,8,64]{5,1,4,2,3,0:T(8,128)(2,1)}, u32[]{:S(2)}) copy-start(bf16[1,16,128,2,8,64]{5,1,4,2,3,0:T(8,128)(2,1)} %copy.43) | copy-start | bytes 12582916
  465.8 8.1 %copy-start.7 = (bf16[512,512]{1,0:T(8,128)(2,1)S(1)}, bf16[512,512]{1,0:T(8,128)(2,1)}, u32[]{:S(2)}) copy-start(bf16[512,512]{1,0:T(8,128)(2,1)} %param.22) | copy-start | bytes 1572868
  473.9 4.4 copy-start.12
  478.3 3.6 copy-start.13
  478.3 3.6 copy-start.9
  478.3 3.6 copy-start.10
  478.8 9.2 %copy-start.8 = (f32[2048]{0:T(1024)}, f32[2048]{0:T(1024)S(1)}, u32[]{:S(2)}) copy-start(f32[2048]{0:T(1024)S(1)} %multiply_reduce_fusion.1) | copy-start | bytes 24580
  478.8 3.1 collective-permute-start.1
where the time goes:
time: 493 us; the launch traced here: 488 us
  local copies, waits for them, and re-layouts  169 us (34%)
  waiting for transfers between devices  153 us (31%)
  matrix products  106 us (22%)
  other arithmetic  37.1 us (8%)
  starting transfers between devices  17.2 us (3%)
    all_to_all x1, waiting for transfers between devices, body(): lax.all_to_all(outgoing, 'agent', split_axis=0, concat_axis=0, tiled=True)  150 us
    dot_general x4, matrix products, agent_group(): jnp.einsum('thqk,tkhe->tqhe', attention, key_part[:, :, 1], preferred_ele...  50 us
    concatenate x2, local copies, waits for them, and re-layouts, body(): jnp.concatenate([keyvals, listed], axis=1)  22.3 us
    unnamed x32, local copies, waits for them, and re-layouts  20.3 us
    sub x5, other arithmetic, softmax_rows(): shifted = scores - jnp.max(scores, axis=-1, keepdims=True)  20.2 us
    while x16, local copies, waits for them, and re-layouts  17.2 us
    dynamic_slice x8, local copies, waits for them, and re-layouts, body(): attended = lax.map(agent_group, (query_heads, all_keys))  14.9 us
    reshape x1, local copies, waits for them, and re-layouts, body(): padded[:steps_here]  13 us
  transfers between devices with their start and end apart: 4, of which 3 were waited for; matrix products, arithmetic and copies ran while one was open for 13% of the time, Pallas kernels for 0%

commit v1 on v0

v1 whole, which is shorter than its diff:
```python
import functools
import math

import jax
import jax.numpy as jnp
from jax import lax
from jax.experimental import pallas as pl
from jax.experimental.pallas import tpu as pltpu
from jax.sharding import PartitionSpec as P

HEADS = 8
WINDOW = 16

discount = 0.9997
trace_decay = 0.995
epsilon = 1e-06
NEG = -1e30
MESH = pl.DeviceIdType.MESH


def normed_bf16(x):
    return (x * lax.rsqrt(jnp.mean(x * x, axis=-1, keepdims=True) + epsilon)).astype(jnp.bfloat16)


def dot(a, b):
    return jnp.dot(a, b, preferred_element_type=jnp.float32)


def pair_attention(q, k, v, head, coef, bias=None):
    rows = q.shape[0]
    first = lax.broadcasted_iota(jnp.int32, q.shape, 1) < head
    zero = jnp.zeros_like(q)
    both = jnp.concatenate([jnp.where(first, q, zero), jnp.where(first, zero, q)], axis=0)
    s = lax.dot_general(both, k, (((1,), (1,)), ((), ())), preferred_element_type=jnp.float32)
    s = s * coef
    if bias is not None:
        s = s + bias
    e = jnp.exp2(s - jnp.max(s, axis=-1, keepdims=True))
    o = dot(e.astype(jnp.bfloat16), v) / jnp.sum(e, axis=-1, keepdims=True)
    return jnp.where(first, o[:rows], o[rows:])


def agent_step(x, listed, proj_ref, merge_ref, tproj_ref, head):
    width = x.shape[-1]
    coef = head**-0.5 * math.log2(math.e)
    x = x.astype(jnp.float32)
    own = dot(normed_bf16(x), proj_ref[...]).astype(jnp.bfloat16)
    other = dot(normed_bf16(listed.astype(jnp.float32)), proj_ref[:, width:]).astype(jnp.bfloat16)
    outs = []
    for lo in range(0, width, 2 * head):
        hi = lo + 2 * head
        k = jnp.concatenate([own[:, width + lo : width + hi], other[:, lo:hi]], axis=0)
        v = jnp.concatenate(
            [own[:, 2 * width + lo : 2 * width + hi], other[:, width + lo : width + hi]], axis=0
        )
        outs.append(pair_attention(own[:, lo:hi], k, v, head, coef))
    mix = jnp.concatenate(outs, axis=1).astype(jnp.bfloat16)
    res = x + dot(mix, merge_ref[...])
    return res, dot(normed_bf16(res), tproj_ref[...]).astype(jnp.bfloat16)


def agent_kernel(head, listing, pos, x_ref, *refs):
    listed = [r[0] for r in refs[:listing]]
    proj, merge, tproj, res_ref, qkv_ref = refs[listing:]
    res, qkv = agent_step(x_ref[0], jnp.concatenate(listed, axis=0), proj, merge, tproj, head)
    res_ref[0] = res
    qkv_ref[0] = qkv


def agent_call(embedded, arrived, positions, proj, merge, tproj, head):
    steps, agents, width = embedded.shape
    listing = positions.shape[0] // steps
    block = (1, agents, width)
    whole = lambda a: pl.BlockSpec(a.shape, lambda t, p: (0, 0))
    pick = lambda j: pl.BlockSpec(block, lambda t, p: (p[t * listing + j], 0, 0))
    return pl.pallas_call(
        functools.partial(agent_kernel, head, listing),
        grid_spec=pltpu.PrefetchScalarGridSpec(
            num_scalar_prefetch=1,
            grid=(steps,),
            in_specs=[pl.BlockSpec(block, lambda t, p: (t, 0, 0))]
            + [pick(j) for j in range(listing)]
            + [whole(proj), whole(merge), whole(tproj)],
            out_specs=[
                pl.BlockSpec(block, lambda t, p: (t, 0, 0)),
                pl.BlockSpec((1, agents, 3 * width), lambda t, p: (t, 0, 0)),
            ],
        ),
        out_shape=[
            jax.ShapeDtypeStruct((steps, agents, width), jnp.float32),
            jax.ShapeDtypeStruct((steps, agents, 3 * width), jnp.bfloat16),
        ],
        compiler_params=pltpu.CompilerParams(vmem_limit_bytes=40 * 2**20),
        name="agent_attention",
    )(positions, embedded, *([arrived] * listing), proj, merge, tproj)


def time_kernel(head, res_ref, qkv_ref, prev_ref, merge_ref, weight_ref, out_ref, mix_ref):
    steps, agents, width = res_ref.shape
    coef = head**-0.5 * math.log2(math.e)
    oct_ = 8
    rows, cols = steps * oct_, 2 * steps * oct_
    r = lax.broadcasted_iota(jnp.int32, (rows, cols), 0)
    c = lax.broadcasted_iota(jnp.int32, (rows, cols), 1)
    qt, ks = r // oct_, c // oct_ - steps
    seen = (ks <= qt) & (ks > qt - WINDOW) & ((ks >= 0) | (lax.axis_index("tm") > 0))
    bias = jnp.where(seen & (r % oct_ == c % oct_), 0.0, NEG).astype(jnp.float32)
    bias = jnp.concatenate([bias, bias], axis=0)

    def halves(block):
        block = block.astype(jnp.float32)
        return [
            block[:, h : h + oct_].reshape(steps * oct_, block.shape[-1]).astype(jnp.bfloat16)
            for h in (0, oct_)
        ]

    def group(i, _):
        at = pl.ds(pl.multiple_of(i * 2 * oct_, 2 * oct_), 2 * oct_)
        for lo in range(0, width, 2 * head):
            hi = lo + 2 * head
            q = halves(qkv_ref[:, at, lo:hi])
            k0 = halves(prev_ref[:, at, lo:hi])
            k1 = halves(qkv_ref[:, at, width + lo : width + hi])
            v0 = halves(prev_ref[:, at, width + lo : width + hi])
            v1 = halves(qkv_ref[:, at, 2 * width + lo : 2 * width + hi])
            outs = []
            for h in range(2):
                k = jnp.concatenate([k0[h], k1[h]], axis=0)
                v = jnp.concatenate([v0[h], v1[h]], axis=0)
                o = pair_attention(q[h], k, v, head, coef, bias)
                outs.append(o.reshape(steps, oct_, hi - lo))
            mix_ref[:, at, lo:hi] = jnp.concatenate(outs, axis=1).astype(jnp.bfloat16)
        return 0

    lax.fori_loop(0, agents // (2 * oct_), group, 0)

    def finish(t, _):
        res = res_ref[t] + dot(mix_ref[t], merge_ref[...])
        square = res * res
        scaled = res * weight_ref[...]
        lanes = 128
        sq = sum(square[:, j : j + lanes] for j in range(0, width, lanes))
        sc = sum(scaled[:, j : j + lanes] for j in range(0, width, lanes))
        mean = jnp.sum(sq.T, axis=0, keepdims=True) / width
        out_ref[pl.ds(t, 1), :] = jnp.sum(sc.T, axis=0, keepdims=True) * lax.rsqrt(mean + epsilon)
        return 0

    lax.fori_loop(0, steps, finish, 0)


def time_call(res, qkv, prev, merge, weight, head):
    steps, agents, width = res.shape
    return pl.pallas_call(
        functools.partial(time_kernel, head),
        out_shape=jax.ShapeDtypeStruct((steps, agents), jnp.float32),
        in_specs=[pl.BlockSpec(memory_space=pltpu.VMEM)] * 5,
        out_specs=pl.BlockSpec(memory_space=pltpu.VMEM),
        scratch_shapes=[pltpu.VMEM((steps, agents, width), jnp.bfloat16)],
        compiler_params=pltpu.CompilerParams(vmem_limit_bytes=56 * 2**20),
        name="time_attention",
    )(res, qkv, prev, merge, weight.reshape(1, width))


def from_behind(value, axis, by):
    devices = lax.axis_size(axis)
    pairs = [(i, i + by) for i in range(devices) if 0 <= i + by < devices]
    return lax.ppermute(value, axis, pairs)


def advantage_pass(values, done_flags, rewards, bootstrap):
    steps = values.shape[0]
    parts = lax.axis_size("tm")
    last = lax.axis_index("tm") == parts - 1
    living = 1.0 - done_flags.astype(jnp.float32)
    factors = discount * trace_decay * living

    def run(following_last, running):
        following = jnp.concatenate([values[1:], following_last[None]], axis=0)
        changes = rewards + discount * living * following - values
        rows = [None] * steps
        for t in reversed(range(steps)):
            running = changes[t] + factors[t] * running
            rows[t] = running
        return jnp.stack(rows)

    zero = jnp.zeros_like(bootstrap)
    advantages = run(bootstrap, zero)
    for _ in range(parts - 1):
        sent = jnp.stack([values[0], advantages[0]])
        got = from_behind(sent, "tm", -1)
        advantages = run(jnp.where(last, bootstrap, got[0]), jnp.where(last, zero, got[1]))
    return advantages


def exchange(embedded, block_lists):
    steps, agents, width = embedded.shape
    listing = block_lists.shape[2]
    blocks = lax.axis_size("agent")
    capacity = max(2, (2 * steps * listing + blocks - 1) // blocks)
    peers = block_lists[0].reshape(-1)
    count = peers.shape[0]
    row_steps = jnp.arange(count, dtype=jnp.int32) // listing
    hits = (peers[:, None] == jnp.arange(blocks, dtype=jnp.int32)[None, :]).astype(jnp.int32)
    earlier = jnp.cumsum(hits, axis=0) - hits
    slot = jnp.sum(earlier * hits, axis=1)
    slots = (slot[:, None] == jnp.arange(capacity, dtype=jnp.int32)[None, :]).astype(jnp.int32)
    requests = jnp.sum((hits * row_steps[:, None])[:, :, None] * slots[:, None, :], axis=0)
    wanted = lax.all_to_all(requests, "agent", split_axis=0, concat_axis=0, tiled=True)
    outgoing = embedded[wanted.reshape(-1)].reshape(blocks, capacity, agents, width)
    arrived = lax.all_to_all(outgoing, "agent", split_axis=0, concat_axis=0, tiled=True)
    return arrived.reshape(blocks * capacity, agents, width), peers * capacity + slot


def body(
    embedded,
    block_lists,
    done_flags,
    rewards,
    bootstrap,
    agent_proj,
    agent_merge,
    time_proj,
    time_merge,
    value_weight,
):
    steps, agents, width = embedded.shape
    head = width // HEADS
    assert steps == WINDOW
    arrived, positions = exchange(embedded, block_lists)
    res, qkv = agent_call(embedded, arrived, positions, agent_proj, agent_merge, time_proj, head)
    prev = from_behind(qkv[:, :, width:], "tm", 1)
    values = time_call(res, qkv, prev, time_merge, value_weight, head)
    return (values, advantage_pass(values, done_flags, rewards, bootstrap))


def solution(mesh):
    placed = (
        P(("groups", "tm"), "agent", None),
        P(("groups", "agent"), "tm", None),
        P(("groups", "tm"), "agent"),
        P(("groups", "tm"), "agent"),
        P(("groups", "agent")),
        P(),
        P(),
        P(),
        P(),
        P(),
    )
    return jax.shard_map(
        body,
        mesh=mesh,
        in_specs=placed,
        out_specs=(P(("groups", "tm"), "agent"), P(("groups", "tm"), "agent")),
        check_vma=False,
    )
```

time: 493 us -> 298 us (0.60)
  local copies, waits for them, and re-layouts: 169 us -> 20 us
  matrix products: 106 us -> 0 us
  Pallas kernels: 0 us -> 61.9 us
  waiting for transfers between devices: 153 us -> 190 us
  other arithmetic: 37.1 us -> 2.74 us
  blocking collectives: 3.6 us -> 13.6 us
  starting transfers between devices: 17.2 us -> 8.06 us
    dot_general x16 -> x0, matrix products: 106 us -> none  [the longest x4 50 us: agent_group(): jnp.einsum('thqk,tkhe->tqhe', attention, key_part[:, :, 1], preferred_ele...]
    pallas_call x0 -> x2, Pallas kernels: none -> 61.9 us  [the longest x1 41.3 us: agent_call(): pl.pallas_call(functools.partial(agent_kernel, head, listing), grid_spec=...]
    reshape x4 -> x1, local copies, waits for them, and re-layouts: 34.8 us -> 0.08 us  [exchange(): wanted.reshape(-1)]
    all_to_all x2 -> x1, waiting for transfers between devices: 151 us -> 182 us  [exchange(): lax.all_to_all(outgoing, 'agent', split_axis=0, concat_axis=0, tiled=True)]
    concatenate x2 -> x0, local copies, waits for them, and re-layouts: 22.3 us -> none  [body(): jnp.concatenate([keyvals, listed], axis=1)]
    sub x5 -> x1, other arithmetic: 20.2 us -> 0.71 us  [run(): changes = rewards + discount * living * following - values]
    convert_element_type x2 -> x0, local copies, waits for them, and re-layouts: 19.4 us -> none  [the longest x1 11.3 us: body(): listed = jnp.dot(listed_rows.reshape(-1, model_width), agent_proj[:, mode...]
    while x16 -> x0, local copies, waits for them, and re-layouts: 17.2 us -> none
  transfers between devices with their start and end apart: 4 -> 3, of which waited for: 3 -> 3; matrix products, arithmetic and copies ran while one was open for 13% -> 0% of each run, Pallas kernels for 0% -> 0%
where the time goes in v1:
time: 298 us; the launch traced here: 297 us
  waiting for transfers between devices  190 us (64%)
  Pallas kernels  61.9 us (21%)
  local copies, waits for them, and re-layouts  20 us (7%)
  blocking collectives  13.6 us (5%)
  starting transfers between devices  8.06 us (3%)
    all_to_all x1, waiting for transfers between devices, exchange(): lax.all_to_all(outgoing, 'agent', split_axis=0, concat_axis=0, tiled=True)  182 us
    pallas_call x1, Pallas kernels, agent_call(): pl.pallas_call(functools.partial(agent_kernel, head, listing), grid_spec=...  41.3 us
    pallas_call x1, Pallas kernels, time_call(): pl.pallas_call(functools.partial(time_kernel, head), out_shape=jax.ShapeD...  20.6 us
    all_to_all x1, blocking collectives, exchange(): lax.all_to_all(requests, 'agent', split_axis=0, concat_axis=0, tiled=True)  13.6 us
    ppermute x2, waiting for transfers between devices, from_behind(): return lax.ppermute(value, axis, pairs)  8.25 us
    gather x1, local copies, waits for them, and re-layouts, exchange(): embedded[wanted.reshape(-1)].reshape(blocks, capacity, agents, width)  6.89 us
  transfers between devices with their start and end apart: 3, of which 3 were waited for; matrix products, arithmetic and copies ran while one was open for 0% of the time, Pallas kernels for 0%

profile of v1, /device:TPU:0, one launch (start us, length us, event | category | flops | bytes accessed | tf_op | source)
XLA Modules:
  0.0 297.1 jit_solution(14432342735975630050)
XLA Ops:
  0.6 0.8 copy.16
  1.4 0.1 reshape_squeeze.3
  1.5 0.1 fusion.1
  1.6 0.1 reduce_window_sum.11
  1.6 0.2 fusion
  1.8 0.1 copy.17
  1.9 0.2 multiply_reduce_fusion
  2.1 13.6 %all_to_all.14 = s32[8,1,8]{2,1,0:T(1,128)S(1)} all-to-all(s32[8,1,8]{2,1,0:T(1,128)S(1)} %bitcast.14), channel_id=1, replica_groups=mesh['groups'=2,'agent'=8,'tm'=2] {'agent'}, dimensions={0} | all-to-all | bytes 512 | tf_op jit(solution)/shard_map/all_to_all | solution.py:208
  15.7 0.5 broadcast.137
  16.2 0.7 reduce.3
  16.9 0.1 reshape.117
  17.0 6.9 %gather_fusion = bf16[64,128,512]{2,1,0:T(8,128)(2,1)} fusion(bf16[16,128,512]{2,1,0:T(8,128)(2,1)} %x_ref.1, s32[1024]{0:T(1024)S(1)} %pad_clamp_fusion), kind=kCustom, calls=%fused_computation | custom fusion | bytes 16777472 | tf_op jit(solution)/shard_map/gather | solution.py:209
  23.9 0.0 copy-start
  23.9 0.0 copy-start.4
  23.9 5.2 %all-to-all-start.1 = ((bf16[8,8,128,512]{3,2,1,0:T(8,128)(2,1)}), bf16[8,8,128,512]{3,2,1,0:T(8,128)(2,1)}, u32[]{:S(2)}, u32[]{:S(2)}) async-start(bf16[8,8,128,512]{3,2,1,0:T(8,128)(2,1)} %bitcast.13), calls=%async_computation.1 | async-start | bytes 16777216 | tf_op jit(solution)/shard_map/all_to_all | solution.py:210
  29.1 181.9 %all-to-all-done.1 = bf16[8,8,128,512]{3,2,1,0:T(8,128)(2,1)} async-done(((bf16[8,8,128,512]{3,2,1,0:T(8,128)(2,1)}), bf16[8,8,128,512]{3,2,1,0:T(8,128)(2,1)}, u32[]{:S(2)}, u32[]{:S(2)}) %all-to-all-start.1) | async-done | bytes 8388640 | tf_op jit(solution)/shard_map/all_to_all | solution.py:210
  211.0 0.0 copy-done
  211.0 0.0 copy-done.4
  211.0 0.0 copy-start.2
  211.0 1.4 copy-done.2
  212.4 0.0 copy-start.3
  212.4 1.4 copy-done.3
  213.8 41.3 %agent_attention.1 = (f32[16,128,512]{2,1,0:T(8,128)S(1)}, bf16[16,128,1536]{2,1,0:T(8,128)(2,1)}) custom-call(s32[32]{0:T(128)S(1)} %multiply_add_fusion.pos, bf16[16,128,512]{2,1,0:T(8,128)(2,1)S(1)} %copy-done, bf16[64,128,512]{2,1,0:T(8,128)(2,1)} %bitcast.4.refs_0_.refs_1_, bf16[64,128,512]{2,1,0:T(8,128)(2,1)} %bitcast.4.refs_0_.refs_1_, ...), custom_call_target="tpu_custom_call" | custom-call | tf_op jit(solution)/shard_map/agent_attention/pallas_call | solution.py:76
  255.1 0.0 copy-start.1
  255.1 4.1 %slice.176 = bf16[16,128,1024]{2,1,0:T(8,128)(2,1)S(1)} slice(bf16[16,128,1536]{2,1,0:T(8,128)(2,1)} %get-tuple-element.5.qkv_ref), slice={[0:16], [0:128], [512:1536]} | slice | bytes 8388608 | tf_op jit(solution)/shard_map/slice | solution.py:231
  259.3 0.0 copy-done.1
  259.3 1.6 collective-permute-start
  260.9 6.5 %collective-permute-done.prev_ref = bf16[16,128,1024]{2,1,0:T(8,128)(2,1)S(1)} collective-permute-done((bf16[16,128,1024]{2,1,0:T(8,128)(2,1)S(1)}, bf16[16,128,1024]{2,1,0:T(8,128)(2,1)S(1)}, u32[]{:S(2)}, u32[]{:S(2)}) %collective-permute-start) | collective-permute-done | bytes 4194336 | tf_op jit(solution)/shard_map/ppermute | solution.py:167
  267.4 0.0 copy-start.5
  267.4 2.0 copy-done.5
  269.3 0.0 copy-start.6
  269.3 0.0 copy-start.7
  269.3 0.0 copy-start.8
  269.3 20.6 %time_attention.1 = f32[16,128]{1,0:T(8,128)} custom-call(f32[16,128,512]{2,1,0:T(8,128)} %copy-done.1, bf16[16,128,1536]{2,1,0:T(8,128)(2,1)} %get-tuple-element.5.qkv_ref, bf16[16,128,1024]{2,1,0:T(8,128)(2,1)} %copy-done.5, bf16[512,512]{1,0:T(8,128)(2,1)} %merge_ref.1, f32[1,512]{1,0:T(1,128)} %bitcast.15), custom_call_target="tpu_custom_call" | custom-call | tf_op jit(solution)/shard_map/time_attention/pallas_call | solution.py:153
  289.9 0.7 slice.231
  290.6 0.7 slice.232
  291.3 0.0 copy-done.6
  291.3 0.0 copy-done.7
  291.3 0.0 copy-done.8
  291.3 0.7 fusion.6
  292.1 1.3 collective-permute-start.1
  293.4 1.8 collective-permute-done.1
  295.1 0.7 fusion.5
  295.9 1.2 stack.5
  (9 shorter events, 0.1 us)
Async XLA Ops:
  23.9 187.1 %copy-start = (bf16[16,128,512]{2,1,0:T(8,128)(2,1)S(1)}, bf16[16,128,512]{2,1,0:T(8,128)(2,1)}, u32[]{:S(2)}) copy-start(bf16[16,128,512]{2,1,0:T(8,128)(2,1)} %x_ref.1) | copy-start | bytes 6291460
  23.9 187.1 %copy-start.4 = (bf16[512,512]{1,0:T(8,128)(2,1)S(1)}, bf16[512,512]{1,0:T(8,128)(2,1)}, u32[]{:S(2)}) copy-start(bf16[512,512]{1,0:T(8,128)(2,1)} %refs_3_.1) | copy-start | bytes 1572868
  23.9 187.1 %all-to-all-start.1 = ((bf16[8,8,128,512]{3,2,1,0:T(8,128)(2,1)}), bf16[8,8,128,512]{3,2,1,0:T(8,128)(2,1)}, u32[]{:S(2)}, u32[]{:S(2)}) async-start(bf16[8,8,128,512]{3,2,1,0:T(8,128)(2,1)} %bitcast.13), calls=%async_computation.1 | async-start | bytes 16777216 | tf_op jit(solution)/shard_map/all_to_all | solution.py:210
  211.0 1.4 copy-start.2
  212.4 1.4 copy-start.3
  255.1 4.1 %copy-start.1 = (f32[16,128,512]{2,1,0:T(8,128)}, f32[16,128,512]{2,1,0:T(8,128)S(1)}, u32[]{:S(2)}) copy-start(f32[16,128,512]{2,1,0:T(8,128)S(1)} %get-tuple-element.4.res_ref) | copy-start | bytes 12582916
  259.3 8.1 %collective-permute-start = (bf16[16,128,1024]{2,1,0:T(8,128)(2,1)S(1)}, bf16[16,128,1024]{2,1,0:T(8,128)(2,1)S(1)}, u32[]{:S(2)}, u32[]{:S(2)}) collective-permute-start(bf16[16,128,1024]{2,1,0:T(8,128)(2,1)S(1)} %slice.176), channel_id=1, source_target_pairs={{0,1},{2,3},{4,5},{6,7},{8,9},{10,11},{12,13},{14,15},{16,17},{18,... | collective-permute-start | bytes 12582920 | tf_op jit(solution)/shard_map/ppermute | solution.py:167
  267.4 2.0 copy-start.5
  269.3 22.0 %copy-start.6 = (f32[16,128]{1,0:T(8,128)S(1)}, f32[16,128]{1,0:T(8,128)}, u32[]{:S(2)}) copy-start(f32[16,128]{1,0:T(8,128)} %param.13) | copy-start | bytes 24580
  269.3 22.0 %copy-start.7 = (s32[16,128]{1,0:T(8,128)S(1)}, s32[16,128]{1,0:T(8,128)}, u32[]{:S(2)}) copy-start(s32[16,128]{1,0:T(8,128)} %param.12) | copy-start | bytes 24580
  269.3 22.0 %copy-start.8 = (f32[128]{0:T(128)S(1)}, f32[128]{0:T(128)}, u32[]{:S(2)}) copy-start(f32[128]{0:T(128)} %param.14) | copy-start | bytes 1540
  292.1 3.1 %collective-permute-start.1 = (f32[2,128]{1,0:T(2,128)S(1)}, f32[2,128]{1,0:T(2,128)S(1)}, u32[]{:S(2)}, u32[]{:S(2)}) collective-permute-start(f32[2,128]{1,0:T(2,128)S(1)} %pad_maximum_fusion), channel_id=1, source_target_pairs={{1,0},{3,2},{5,4},{7,6},{9,8},{11,10},{13,12},{15,14},{17,16},{19,... | collective-permute-start | bytes 3080 | tf_op jit(solution)/shard_map/ppermute | solution.py:167

commit v2 on v1

--- a/solution.py
+++ b/solution.py
@@ -211,6 +211,170 @@
     return arrived.reshape(blocks * capacity, agents, width), peers * capacity + slot
 
 
+LEAD = 2
+
+
+def row_gather_kernel(
+    head, x_ref, mine_ref, theirs_ref, proj, merge, tproj, res_ref, qkv_ref,
+    row, yout, yin, send_sem, recv_sem, ysend, yrecv,
+):
+    steps = x_ref.shape[0]
+    listing = mine_ref.shape[1]
+    lines = row.shape[0]
+    me = lax.axis_index("agent")
+    y = lax.rem(me, 2)
+    z = lax.div(me, 2)
+    across = me + 1 - 2 * y
+    has_up, has_down = z < lines - 1, z > 0
+    up, down = {"agent": me + 2}, {"agent": me - 2}
+
+    barrier = pltpu.get_barrier_semaphore()
+    pl.semaphore_signal(barrier, inc=1, device_id={"agent": across}, device_id_type=MESH)
+
+    @pl.when(has_up)
+    def _():
+        pl.semaphore_signal(barrier, inc=1, device_id=up, device_id_type=MESH)
+
+    @pl.when(has_down)
+    def _():
+        pl.semaphore_signal(barrier, inc=1, device_id=down, device_id_type=MESH)
+
+    pl.semaphore_wait(barrier, 1 + has_up.astype(jnp.int32) + has_down.astype(jnp.int32))
+
+    def hop(way, h, c, own=False):
+        origin = z - h if way == 0 else z + h
+        return pltpu.make_async_remote_copy(
+            src_ref=x_ref.at[c] if own else row.at[origin, c],
+            dst_ref=row.at[origin, c],
+            send_sem=send_sem.at[way, h, c],
+            recv_sem=recv_sem.at[way, h, c],
+            device_id=up if way == 0 else down,
+            device_id_type=MESH,
+        )
+
+    def arrival(way, h, c):
+        origin = z - h if way == 0 else z + h
+        return pltpu.make_async_remote_copy(
+            src_ref=row.at[origin, c],
+            dst_ref=row.at[origin, c],
+            send_sem=send_sem.at[way, h - 1, c],
+            recv_sem=recv_sem.at[way, h - 1, c],
+            device_id={"agent": across},
+            device_id_type=MESH,
+        )
+
+    def crossing(c):
+        return pltpu.make_async_remote_copy(
+            src_ref=yout.at[c],
+            dst_ref=yin.at[c],
+            send_sem=ysend.at[c],
+            recv_sem=yrecv.at[c],
+            device_id={"agent": across},
+            device_id_type=MESH,
+        )
+
+    def held(way, h):
+        return z >= h if way == 0 else z + h < lines
+
+    def sends(way, h):
+        return held(way, h) & (has_up if way == 0 else has_down)
+
+    def start_own(c):
+        for way in range(2):
+            @pl.when(sends(way, 0) & (c < steps))
+            def _(way=way):
+                hop(way, 0, c, own=True).start()
+
+    for c in range(LEAD):
+        start_own(c)
+
+    def fill(t, _):
+        row[z, t] = x_ref[t]
+        return 0
+
+    lax.fori_loop(0, steps, fill, 0)
+
+    def pick(idx, t, other):
+        for zz in range(lines):
+            other = jnp.where(idx == 2 * zz + y, row[zz, t], other)
+        return other
+
+    def iteration(i, _):
+        start_own(i + LEAD)
+        for h in range(1, lines):
+            c = i - h
+            for way in range(2):
+                @pl.when((c >= 0) & (c < steps) & held(way, h))
+                def _(way=way, h=h, c=c):
+                    arrival(way, h, c).wait_recv()
+
+                if h < lines - 1:
+                    @pl.when((c >= 0) & (c < steps) & sends(way, h))
+                    def _(way=way, h=h, c=c):
+                        hop(way, h, c).start()
+        c = i - (lines - 1)
+
+        @pl.when((c >= 0) & (c < steps))
+        def _():
+            for j in range(listing):
+                yout[c, j] = pick(theirs_ref[c, j], c, row[0, c])
+            crossing(c).start()
+
+        t = i - lines
+
+        @pl.when((t >= 0) & (t < steps))
+        def _():
+            crossing(t).wait_recv()
+            listed = [pick(mine_ref[t, j], t, yin[t, j]) for j in range(listing)]
+            res, qkv = agent_step(x_ref[t], jnp.concatenate(listed, axis=0), proj, merge, tproj, head)
+            res_ref[t] = res
+            qkv_ref[t] = qkv
+
+        return 0
+
+    lax.fori_loop(0, steps + lines, iteration, 0)
+
+    def drain(c, _):
+        crossing(c).wait_send()
+        for way in range(2):
+            for h in range(lines - 1):
+                @pl.when(sends(way, h))
+                def _(way=way, h=h):
+                    hop(way, h, c, own=h == 0).wait_send()
+        return 0
+
+    lax.fori_loop(0, steps, drain, 0)
+
+
+def row_gather_call(embedded, mine, theirs, proj, merge, tproj, head):
+    steps, agents, width = embedded.shape
+    lines = lax.axis_size("agent") // 2
+    listing = mine.shape[1]
+    vmem, smem = pl.BlockSpec(memory_space=pltpu.VMEM), pl.BlockSpec(memory_space=pltpu.SMEM)
+    return pl.pallas_call(
+        functools.partial(row_gather_kernel, head),
+        in_specs=[vmem, smem, smem, vmem, vmem, vmem],
+        out_specs=[vmem, vmem],
+        out_shape=[
+            jax.ShapeDtypeStruct((steps, agents, width), jnp.float32),
+            jax.ShapeDtypeStruct((steps, agents, 3 * width), jnp.bfloat16),
+        ],
+        scratch_shapes=[
+            pltpu.VMEM((lines, steps, agents, width), jnp.bfloat16),
+            pltpu.VMEM((steps, listing, agents, width), jnp.bfloat16),
+            pltpu.VMEM((steps, listing, agents, width), jnp.bfloat16),
+            pltpu.SemaphoreType.DMA((2, lines - 1, steps)),
+            pltpu.SemaphoreType.DMA((2, lines - 1, steps)),
+            pltpu.SemaphoreType.DMA((steps,)),
+            pltpu.SemaphoreType.DMA((steps,)),
+        ],
+        compiler_params=pltpu.CompilerParams(
+            collective_id=0, has_side_effects=True, vmem_limit_bytes=58 * 2**20
+        ),
+        name="row_gather_attention",
+    )(embedded, mine, theirs, proj, merge, tproj)
+
+
 def body(
     embedded,
     block_lists,
@@ -226,8 +390,18 @@
     steps, agents, width = embedded.shape
     head = width // HEADS
     assert steps == WINDOW
-    arrived, positions = exchange(embedded, block_lists)
-    res, qkv = agent_call(embedded, arrived, positions, agent_proj, agent_merge, time_proj, head)
+    blocks = lax.axis_size("agent")
+    gathered = (blocks // 2) * steps * agents * width * 2
+    if blocks % 2 == 0 and blocks > 2 and gathered <= 12 * 2**20:
+        theirs = lax.ppermute(block_lists[0], "agent", [(i, i ^ 1) for i in range(blocks)])
+        res, qkv = row_gather_call(
+            embedded, block_lists[0], theirs, agent_proj, agent_merge, time_proj, head
+        )
+    else:
+        arrived, positions = exchange(embedded, block_lists)
+        res, qkv = agent_call(
+            embedded, arrived, positions, agent_proj, agent_merge, time_proj, head
+        )
     prev = from_behind(qkv[:, :, width:], "tm", 1)
     values = time_call(res, qkv, prev, time_merge, value_weight, head)
     return (values, advantage_pass(values, done_flags, rewards, bootstrap))

time: 298 us -> 208 us (0.70)
  waiting for transfers between devices: 190 us -> 9.88 us
  Pallas kernels: 61.9 us -> 181 us
  blocking collectives: 13.6 us -> 0 us
  local copies, waits for them, and re-layouts: 20 us -> 8.66 us
    all_to_all x1 -> x0, waiting for transfers between devices: 182 us -> none  [exchange(): lax.all_to_all(outgoing, 'agent', split_axis=0, concat_axis=0, tiled=True)]
    pallas_call x1, Pallas kernels: 41.3 us -> 160 us  [row_gather_call(): pl.pallas_call(functools.partial(row_gather_kernel, head), in_specs=[vmem...]
    all_to_all x1 -> x0, blocking collectives: 13.6 us -> none  [exchange(): lax.all_to_all(requests, 'agent', split_axis=0, concat_axis=0, tiled=True)]
    gather x1 -> x0, local copies, waits for them, and re-layouts: 6.89 us -> none  [exchange(): embedded[wanted.reshape(-1)].reshape(blocks, capacity, agents, width)]
    all_to_all x1 -> x0, starting transfers between devices: 5.21 us -> none  [exchange(): lax.all_to_all(outgoing, 'agent', split_axis=0, concat_axis=0, tiled=True)]
    ppermute x0 -> x1, starting transfers between devices: none -> 3 us  [body(): lax.ppermute(block_lists[0], 'agent', [(i, i ^ 1) for i in range(blocks)])]
where the time goes in v2:
time: 208 us; the launch traced here: 207 us
  Pallas kernels  181 us (87%)
  waiting for transfers between devices  9.88 us (5%)
  local copies, waits for them, and re-layouts  8.66 us (4%)
  starting transfers between devices  5.84 us (3%)
    pallas_call x1, Pallas kernels, row_gather_call(): pl.pallas_call(functools.partial(row_gather_kernel, head), in_specs=[vmem...  160 us
    pallas_call x1, Pallas kernels, time_call(): pl.pallas_call(functools.partial(time_kernel, head), out_shape=jax.ShapeD...  20.6 us
    ppermute x2, waiting for transfers between devices, from_behind(): return lax.ppermute(value, axis, pairs)  8.25 us
  transfers between devices with their start and end apart: 3, of which 3 were waited for; matrix products, arithmetic and copies ran while one was open for 0% of the time, Pallas kernels for 0%

profile of v2, /device:TPU:0, one launch (start us, length us, event | category | flops | bytes accessed | tf_op | source)
XLA Modules:
  0.0 207.1 jit_solution(12213019099136108741)
XLA Ops:
  0.6 0.8 copy.13.mine_ref
  1.4 0.0 copy-start.1
  1.4 3.0 %collective-permute-start = (s32[16,2]{1,0:T(8,128)S(1)}, s32[16,2]{1,0:T(8,128)S(1)}, u32[]{:S(2)}, u32[]{:S(2)}) collective-permute-start(s32[16,2]{1,0:T(8,128)S(1)} %copy.13.mine_ref), channel_id=1, source_target_pairs={{0,2},{2,0},{4,6},{6,4},{8,10},{10,8},{12,14},{14,12},{1,3},{3,1},... | collective-permute-start | bytes 392 | tf_op jit(solution)/shard_map/ppermute | solution.py:396
  4.4 1.6 collective-permute-done.theirs_ref
  6.0 0.0 copy-done.1
  6.0 0.0 copy-start.4
  6.0 0.6 copy-done.4
  6.6 160.0 %row_gather_attention.1 = (f32[16,128,512]{2,1,0:T(8,128)}, bf16[16,128,1536]{2,1,0:T(8,128)(2,1)}) custom-call(bf16[16,128,512]{2,1,0:T(8,128)(2,1)} %x_ref.1, s32[16,2]{1,0:T(8,128)} %copy-done.1, s32[16,2]{1,0:T(8,128)} %copy-done.4, bf16[512,1536]{1,0:T(8,128)(2,1)} %proj.1, bf16[512,512]{1,0:T(8,128)(2,1)} %merge.1, bf16[512,1536]{1,0:T(8,128)(2,1)} %tproj.1), custom_call_target="tpu_custom_call" | custom-call | tf_op jit(solution)/shard_map/row_gather_attention/pallas_call | solution.py:354
  166.6 2.6 %slice.176 = bf16[16,128,1024]{2,1,0:T(8,128)(2,1)S(1)} slice(bf16[16,128,1536]{2,1,0:T(8,128)(2,1)} %get-tuple-element.5.qkv_ref), slice={[0:16], [0:128], [512:1536]} | slice | bytes 8388608 | tf_op jit(solution)/shard_map/slice | solution.py:405
  169.2 1.6 collective-permute-start.1
  170.8 6.5 %collective-permute-done.1.prev_ref = bf16[16,128,1024]{2,1,0:T(8,128)(2,1)S(1)} collective-permute-done((bf16[16,128,1024]{2,1,0:T(8,128)(2,1)S(1)}, bf16[16,128,1024]{2,1,0:T(8,128)(2,1)S(1)}, u32[]{:S(2)}, u32[]{:S(2)}) %collective-permute-start.1) | collective-permute-done | bytes 4194336 | tf_op jit(solution)/shard_map/ppermute | solution.py:167
  177.3 0.0 copy-start
  177.3 2.1 copy-done
  179.4 0.0 copy-start.2
  179.4 0.0 copy-start.3
  179.4 0.0 copy-start.5
  179.4 20.6 %time_attention.1 = f32[16,128]{1,0:T(8,128)} custom-call(f32[16,128,512]{2,1,0:T(8,128)} %get-tuple-element.4.res_ref, bf16[16,128,1536]{2,1,0:T(8,128)(2,1)} %get-tuple-element.5.qkv_ref, bf16[16,128,1024]{2,1,0:T(8,128)(2,1)} %copy-done, bf16[512,512]{1,0:T(8,128)(2,1)} %merge_ref.1, f32[1,512]{1,0:T(1,128)} %bitcast.7), custom_call_target="tpu_custom_call" | custom-call | tf_op jit(solution)/shard_map/time_attention/pallas_call | solution.py:153
  199.9 0.7 slice.229
  200.6 0.7 slice.230
  201.3 0.0 copy-done.2
  201.3 0.0 copy-done.3
  201.3 0.0 copy-done.5
  201.3 0.7 fusion.4
  202.1 1.3 collective-permute-start.2
  203.4 1.8 collective-permute-done.2
  205.2 0.7 fusion.3
  205.9 1.2 stack.5
  (4 shorter events, 0.1 us)
Async XLA Ops:
  1.4 4.6 %copy-start.1 = (s32[16,2]{1,0:T(8,128)}, s32[16,2]{1,0:T(8,128)S(1)}, u32[]{:S(2)}) copy-start(s32[16,2]{1,0:T(8,128)S(1)} %copy.13.mine_ref) | copy-start | bytes 388
  1.4 4.6 %collective-permute-start = (s32[16,2]{1,0:T(8,128)S(1)}, s32[16,2]{1,0:T(8,128)S(1)}, u32[]{:S(2)}, u32[]{:S(2)}) collective-permute-start(s32[16,2]{1,0:T(8,128)S(1)} %copy.13.mine_ref), channel_id=1, source_target_pairs={{0,2},{2,0},{4,6},{6,4},{8,10},{10,8},{12,14},{14,12},{1,3},{3,1},... | collective-permute-start | bytes 392 | tf_op jit(solution)/shard_map/ppermute | solution.py:396
  6.0 0.6 copy-start.4
  169.2 8.1 %collective-permute-start.1 = (bf16[16,128,1024]{2,1,0:T(8,128)(2,1)S(1)}, bf16[16,128,1024]{2,1,0:T(8,128)(2,1)S(1)}, u32[]{:S(2)}, u32[]{:S(2)}) collective-permute-start(bf16[16,128,1024]{2,1,0:T(8,128)(2,1)S(1)} %slice.176), channel_id=1, source_target_pairs={{0,1},{2,3},{4,5},{6,7},{8,9},{10,11},{12,13},{14,15},{16,17},{18,... | collective-permute-start | bytes 12582920 | tf_op jit(solution)/shard_map/ppermute | solution.py:167
  177.3 2.1 copy-start
  179.4 22.0 %copy-start.2 = (f32[16,128]{1,0:T(8,128)S(1)}, f32[16,128]{1,0:T(8,128)}, u32[]{:S(2)}) copy-start(f32[16,128]{1,0:T(8,128)} %param.13) | copy-start | bytes 24580
  179.4 22.0 %copy-start.3 = (s32[16,128]{1,0:T(8,128)S(1)}, s32[16,128]{1,0:T(8,128)}, u32[]{:S(2)}) copy-start(s32[16,128]{1,0:T(8,128)} %param.12) | copy-start | bytes 24580
  179.4 22.0 %copy-start.5 = (f32[128]{0:T(128)S(1)}, f32[128]{0:T(128)}, u32[]{:S(2)}) copy-start(f32[128]{0:T(128)} %param.14) | copy-start | bytes 1540
  202.1 3.1 %collective-permute-start.2 = (f32[2,128]{1,0:T(2,128)S(1)}, f32[2,128]{1,0:T(2,128)S(1)}, u32[]{:S(2)}, u32[]{:S(2)}) collective-permute-start(f32[2,128]{1,0:T(2,128)S(1)} %pad_maximum_fusion), channel_id=1, source_target_pairs={{1,0},{3,2},{5,4},{7,6},{9,8},{11,10},{13,12},{15,14},{17,16},{19,... | collective-permute-start | bytes 3080 | tf_op jit(solution)/shard_map/ppermute | solution.py:167

commit v3 on v2

--- a/solution.py
+++ b/solution.py
@@ -211,13 +211,19 @@
     return arrived.reshape(blocks * capacity, agents, width), peers * capacity + slot
 
 
-LEAD = 2
+LEAD = 4
+QUERY_STEPS = 4
 
 
 def row_gather_kernel(
-    head, x_ref, mine_ref, theirs_ref, proj, merge, tproj, res_ref, qkv_ref,
-    row, yout, yin, send_sem, recv_sem, ysend, yrecv,
+    head, x_ref, mine_ref, theirs_ref, proj, merge, tproj, tmerge, weight_ref,
+    done_ref, reward_ref, boot_ref, values_ref, adv_ref,
+    row, yout, yin, res_ref, q_ref, kv_ref, mix_ref, edge_out, edge_in,
+    send_sem, recv_sem, ysend, yrecv, kvsend, kvrecv, edge_sem, go_sem,
 ):
+    agents, width = x_ref.shape[1:]
+    tm = lax.axis_index("tm")
+    earlier, later = tm > 0, tm < lax.axis_size("tm") - 1
     steps = x_ref.shape[0]
     listing = mine_ref.shape[1]
     lines = row.shape[0]
@@ -239,7 +245,16 @@
     def _():
         pl.semaphore_signal(barrier, inc=1, device_id=down, device_id_type=MESH)
 
-    pl.semaphore_wait(barrier, 1 + has_up.astype(jnp.int32) + has_down.astype(jnp.int32))
+    @pl.when(earlier)
+    def _():
+        pl.semaphore_signal(barrier, inc=1, device_id={"tm": tm - 1}, device_id_type=MESH)
+
+    @pl.when(later)
+    def _():
+        pl.semaphore_signal(barrier, inc=1, device_id={"tm": tm + 1}, device_id_type=MESH)
+
+    friends = [has_up, has_down, earlier, later]
+    pl.semaphore_wait(barrier, 1 + sum(friend.astype(jnp.int32) for friend in friends))
 
     def hop(way, h, c, own=False):
         origin = z - h if way == 0 else z + h
@@ -285,14 +300,89 @@
             def _(way=way):
                 hop(way, 0, c, own=True).start()
 
+    def kv_copy(t):
+        return pltpu.make_async_remote_copy(
+            src_ref=kv_ref.at[steps + t],
+            dst_ref=kv_ref.at[t],
+            send_sem=kvsend.at[t],
+            recv_sem=kvrecv.at[t],
+            device_id={"tm": lax.rem(tm + 1, lax.axis_size("tm"))},
+            device_id_type=MESH,
+        )
+
+    def edge_copy():
+        count = lax.axis_size("tm")
+        return pltpu.make_async_remote_copy(
+            src_ref=edge_out,
+            dst_ref=edge_in,
+            send_sem=edge_sem.at[0],
+            recv_sem=edge_sem.at[1],
+            device_id={"tm": lax.rem(tm + count - 1, count)},
+            device_id_type=MESH,
+        )
+
+    def fill(t, _):
+        row[z, t] = x_ref[t]
+
+        @pl.when(jnp.logical_not(earlier))
+        def _():
+            kv_ref[t] = jnp.zeros(kv_ref.shape[1:], kv_ref.dtype)
+
+        return 0
+
+    lax.fori_loop(0, steps, fill, 0)
+
+    @pl.when(earlier)
+    def _():
+        pl.semaphore_wait(go_sem, 1)
+
     for c in range(LEAD):
         start_own(c)
 
-    def fill(t, _):
-        row[z, t] = x_ref[t]
-        return 0
-
-    lax.fori_loop(0, steps, fill, 0)
+    oct_, qs = 8, QUERY_STEPS
+    ks = qs + steps
+    coef = head**-0.5 * math.log2(math.e)
+
+    def halves(block):
+        block = block.astype(jnp.float32)
+        return [
+            block[:, h : h + oct_].reshape(-1, block.shape[-1]).astype(jnp.bfloat16)
+            for h in (0, oct_)
+        ]
+
+    def time_chunk(q0):
+        r = lax.broadcasted_iota(jnp.int32, (qs * oct_, ks * oct_), 0)
+        c = lax.broadcasted_iota(jnp.int32, (qs * oct_, ks * oct_), 1)
+        ahead = c // oct_ - r // oct_
+        seen = (ahead > 0) & (ahead <= WINDOW) & ((q0 + c // oct_ >= steps) | earlier)
+        bias = jnp.where(seen & (r % oct_ == c % oct_), 0.0, NEG).astype(jnp.float32)
+        bias = jnp.concatenate([bias, bias], axis=0)
+
+        def group(i, _):
+            at = pl.ds(pl.multiple_of(i * 2 * oct_, 2 * oct_), 2 * oct_)
+            for lo in range(0, width, 2 * head):
+                hi = lo + 2 * head
+                q = halves(q_ref[pl.ds(q0, qs), at, lo:hi])
+                k = halves(kv_ref[pl.ds(q0, ks), at, lo:hi])
+                v = halves(kv_ref[pl.ds(q0, ks), at, width + lo : width + hi])
+                outs = [
+                    pair_attention(q[h], k[h], v[h], head, coef, bias).reshape(qs, oct_, hi - lo)
+                    for h in range(2)
+                ]
+                mix_ref[:, at, lo:hi] = jnp.concatenate(outs, axis=1).astype(jnp.bfloat16)
+            return 0
+
+        lax.fori_loop(0, agents // (2 * oct_), group, 0)
+        mixed = dot(mix_ref[...].reshape(qs * agents, width), tmerge[...])
+        lanes = 128
+        for j in range(qs):
+            res = res_ref[q0 + j] + mixed[j * agents : (j + 1) * agents]
+            square, scaled = res * res, res * weight_ref[...]
+            sq = sum(square[:, lo : lo + lanes] for lo in range(0, width, lanes))
+            sc = sum(scaled[:, lo : lo + lanes] for lo in range(0, width, lanes))
+            mean = jnp.sum(sq.T, axis=0, keepdims=True) / width
+            value = jnp.sum(sc.T, axis=0, keepdims=True) * lax.rsqrt(mean + epsilon)
+            values_ref[pl.ds(q0 + j, 1), :] = value
 
     def pick(idx, t, other):
         for zz in range(lines):
@@ -324,18 +414,72 @@
 
         @pl.when((t >= 0) & (t < steps))
         def _():
+            @pl.when(later & (t > 0))
+            def _():
+                kv_copy(t - 1).start()
+
             crossing(t).wait_recv()
             listed = [pick(mine_ref[t, j], t, yin[t, j]) for j in range(listing)]
             res, qkv = agent_step(x_ref[t], jnp.concatenate(listed, axis=0), proj, merge, tproj, head)
             res_ref[t] = res
-            qkv_ref[t] = qkv
+            q_ref[t] = qkv[:, :width]
+            kv_ref[steps + t] = qkv[:, width:]
+
+            @pl.when(earlier & (t == 0))
+            def _():
+                def ready(s, _):
+                    kv_copy(s).wait_recv()
+                    return 0
+
+                lax.fori_loop(0, steps, ready, 0)
+
+            @pl.when(lax.rem(t, qs) == qs - 1)
+            def _():
+                time_chunk(t - (qs - 1))
+
+        @pl.when(later & (i == steps - LEAD))
+        def _():
+            pl.semaphore_signal(go_sem, inc=1, device_id={"tm": tm + 1}, device_id_type=MESH)
 
         return 0
 
     lax.fori_loop(0, steps + lines, iteration, 0)
+
+    @pl.when(later)
+    def _():
+        kv_copy(steps - 1).start()
+        edge_copy().wait_recv()
+        edge_out[...] = edge_in[...]
+
+    @pl.when(jnp.logical_not(later))
+    def _():
+        edge_out[0:1, :] = boot_ref[...]
+        edge_out[1:2, :] = jnp.zeros_like(boot_ref)
+
+    value, running = edge_out[0:1, :], edge_out[1:2, :]
+    rows = []
+    for t in reversed(range(steps)):
+        living = 1.0 - done_ref[t : t + 1, :].astype(jnp.float32)
+        following, value = value, values_ref[t : t + 1, :]
+        change = reward_ref[t : t + 1, :] + discount * living * following - value
+        running = change + discount * trace_decay * living * running
+        rows.append(running)
+    edge_out[0:1, :] = value
+    edge_out[1:2, :] = running
+    for t in range(steps):
+        adv_ref[t : t + 1, :] = rows[steps - 1 - t]
+
+    @pl.when(earlier)
+    def _():
+        edge_copy().start()
 
     def drain(c, _):
         crossing(c).wait_send()
+
+        @pl.when(later)
+        def _():
+            kv_copy(c).wait_send()
+
         for way in range(2):
             for h in range(lines - 1):
                 @pl.when(sends(way, h))
@@ -345,34 +489,52 @@
 
     lax.fori_loop(0, steps, drain, 0)
 
-
-def row_gather_call(embedded, mine, theirs, proj, merge, tproj, head):
+    @pl.when(earlier)
+    def _():
+        edge_copy().wait_send()
+
+
+def row_gather_call(
+    embedded, mine, theirs, proj, merge, tproj, tmerge, weight, done, rewards, bootstrap, head
+):
     steps, agents, width = embedded.shape
     lines = lax.axis_size("agent") // 2
     listing = mine.shape[1]
     vmem, smem = pl.BlockSpec(memory_space=pltpu.VMEM), pl.BlockSpec(memory_space=pltpu.SMEM)
+    dma = pltpu.SemaphoreType.DMA
+    out = jax.ShapeDtypeStruct((steps, agents), jnp.float32)
     return pl.pallas_call(
         functools.partial(row_gather_kernel, head),
-        in_specs=[vmem, smem, smem, vmem, vmem, vmem],
+        in_specs=[vmem, smem, smem] + [vmem] * 8,
         out_specs=[vmem, vmem],
-        out_shape=[
-            jax.ShapeDtypeStruct((steps, agents, width), jnp.float32),
-            jax.ShapeDtypeStruct((steps, agents, 3 * width), jnp.bfloat16),
-        ],
+        out_shape=[out, out],
         scratch_shapes=[
             pltpu.VMEM((lines, steps, agents, width), jnp.bfloat16),
             pltpu.VMEM((steps, listing, agents, width), jnp.bfloat16),
             pltpu.VMEM((steps, listing, agents, width), jnp.bfloat16),
-            pltpu.SemaphoreType.DMA((2, lines - 1, steps)),
-            pltpu.SemaphoreType.DMA((2, lines - 1, steps)),
-            pltpu.SemaphoreType.DMA((steps,)),
-            pltpu.SemaphoreType.DMA((steps,)),
+            pltpu.VMEM((steps, agents, width), jnp.float32),
+            pltpu.VMEM((steps, agents, width), jnp.bfloat16),
+            pltpu.VMEM((2 * steps, agents, 2 * width), jnp.bfloat16),
+            pltpu.VMEM((QUERY_STEPS, agents, width), jnp.bfloat16),
+            pltpu.VMEM((2, agents), jnp.float32),
+            pltpu.VMEM((2, agents), jnp.float32),
+            dma((2, lines - 1, steps)),
+            dma((2, lines - 1, steps)),
+            dma((steps,)),
+            dma((steps,)),
+            dma((steps,)),
+            dma((steps,)),
+            dma((2,)),
+            pltpu.SemaphoreType.REGULAR,
         ],
         compiler_params=pltpu.CompilerParams(
             collective_id=0, has_side_effects=True, vmem_limit_bytes=58 * 2**20
         ),
-        name="row_gather_attention",
-    )(embedded, mine, theirs, proj, merge, tproj)
+        name="critic_layer",
+    )(
+        embedded, mine, theirs, proj, merge, tproj, tmerge, weight.reshape(1, width),
+        done, rewards, bootstrap.reshape(1, agents),
+    )
 
 
 def body(
@@ -394,14 +556,13 @@
     gathered = (blocks // 2) * steps * agents * width * 2
     if blocks % 2 == 0 and blocks > 2 and gathered <= 12 * 2**20:
         theirs = lax.ppermute(block_lists[0], "agent", [(i, i ^ 1) for i in range(blocks)])
-        res, qkv = row_gather_call(
-            embedded, block_lists[0], theirs, agent_proj, agent_merge, time_proj, head
-        )
-    else:
-        arrived, positions = exchange(embedded, block_lists)
-        res, qkv = agent_call(
-            embedded, arrived, positions, agent_proj, agent_merge, time_proj, head
-        )
+        values, advantages = row_gather_call(
+            embedded, block_lists[0], theirs, agent_proj, agent_merge, time_proj, time_merge,
+            value_weight, done_flags, rewards, bootstrap, head,
+        )
+        return (values, advantages)
+    arrived, positions = exchange(embedded, block_lists)
+    res, qkv = agent_call(embedded, arrived, positions, agent_proj, agent_merge, time_proj, head)
     prev = from_behind(qkv[:, :, width:], "tm", 1)
     values = time_call(res, qkv, prev, time_merge, value_weight, head)
     return (values, advantage_pass(values, done_flags, rewards, bootstrap))

time: 208 us -> 301 us (1.45)
  Pallas kernels: 181 us -> 291 us
  waiting for transfers between devices: 9.88 us -> 1.63 us
  local copies, waits for them, and re-layouts: 8.66 us -> 3.95 us
    pallas_call x1, Pallas kernels: 160 us -> 291 us  [row_gather_call(): pl.pallas_call(functools.partial(row_gather_kernel, head), in_specs=[vmem...]
    pallas_call x1 -> x0, Pallas kernels: 20.6 us -> none  [time_call(): pl.pallas_call(functools.partial(time_kernel, head), out_shape=jax.ShapeD...]
    ppermute x2 -> x0, waiting for transfers between devices: 8.25 us -> none  [from_behind(): return lax.ppermute(value, axis, pairs)]
    slice x3 -> x0, local copies, waits for them, and re-layouts: 4.02 us -> none  [the longest x1 2.63 us: body(): prev = from_behind(qkv[:, :, width:], 'tm', 1)]
  transfers between devices with their start and end apart: 3 -> 1, of which waited for: 3 -> 1; matrix products, arithmetic and copies ran while one was open for 0% -> 0% of each run, Pallas kernels for 0% -> 0%
where the time goes in v3:
time: 301 us
  Pallas kernels  291 us (97%)
  local copies, waits for them, and re-layouts  3.95 us (1%)
    pallas_call x1, Pallas kernels, row_gather_call(): pl.pallas_call(functools.partial(row_gather_kernel, head), in_specs=[vmem...  291 us
  transfers between devices with their start and end apart: 1, of which 1 were waited for; matrix products, arithmetic and copies ran while one was open for 0% of the time, Pallas kernels for 0%

profile of v3, /device:TPU:0, one launch (start us, length us, event | category | flops | bytes accessed | tf_op | source)
XLA Modules:
  0.0 300.6 jit_solution(15432503204973004437)
XLA Ops:
  0.6 0.8 copy.13.mine_ref
  1.4 0.0 copy-start
  1.4 3.0 collective-permute-start
  4.4 1.6 collective-permute-done.theirs_ref
  6.0 0.0 copy-start.1
  6.0 0.0 copy-done
  6.0 0.6 copy-done.1
  6.6 291.4 %critic_layer.1 = (f32[16,128]{1,0:T(8,128)}, f32[16,128]{1,0:T(8,128)}) custom-call(bf16[16,128,512]{2,1,0:T(8,128)(2,1)} %x_ref.1, s32[16,2]{1,0:T(8,128)} %copy-done, s32[16,2]{1,0:T(8,128)} %copy-done.1, bf16[512,1536]{1,0:T(8,128)(2,1)} %proj.1, bf16[512,512]{1,0:T(8,128)(2,1)} %merge.1, bf16[512,1536]{1,0:T(8,128)(2,1)} %tproj.1, ...), custom_call_target="tpu_custom_call" | custom-call | tf_op jit(solution)/shard_map/critic_layer/pallas_call | solution.py:506
  298.0 1.3 copy.16
  299.3 1.3 copy.17
Async XLA Ops:
  1.4 4.6 %copy-start = (s32[16,2]{1,0:T(8,128)}, s32[16,2]{1,0:T(8,128)S(1)}, u32[]{:S(2)}) copy-start(s32[16,2]{1,0:T(8,128)S(1)} %copy.13.mine_ref) | copy-start | bytes 388
  1.4 4.6 %collective-permute-start = (s32[16,2]{1,0:T(8,128)S(1)}, s32[16,2]{1,0:T(8,128)S(1)}, u32[]{:S(2)}, u32[]{:S(2)}) collective-permute-start(s32[16,2]{1,0:T(8,128)S(1)} %copy.13.mine_ref), channel_id=1, source_target_pairs={{0,2},{2,0},{4,6},{6,4},{8,10},{10,8},{12,14},{14,12},{1,3},{3,1},... | collective-permute-start | bytes 392 | tf_op jit(solution)/shard_map/ppermute | solution.py:558
  6.0 0.6 copy-start.1

commit v4 on v3

--- a/solution.py
+++ b/solution.py
@@ -212,14 +212,14 @@
 
 
 LEAD = 4
-QUERY_STEPS = 4
+QUERY_STEPS = 16
 
 
 def row_gather_kernel(
     head, x_ref, mine_ref, theirs_ref, proj, merge, tproj, tmerge, weight_ref,
     done_ref, reward_ref, boot_ref, values_ref, adv_ref,
     row, yout, yin, res_ref, q_ref, kv_ref, mix_ref, edge_out, edge_in,
-    send_sem, recv_sem, ysend, yrecv, kvsend, kvrecv, edge_sem, go_sem,
+    send_sem, recv_sem, ysend, yrecv, kvsend, kvrecv, edge_sem,
 ):
     agents, width = x_ref.shape[1:]
     tm = lax.axis_index("tm")
@@ -332,10 +332,6 @@
 
     lax.fori_loop(0, steps, fill, 0)
 
-    @pl.when(earlier)
-    def _():
-        pl.semaphore_wait(go_sem, 1)
-
     for c in range(LEAD):
         start_own(c)
 
@@ -425,22 +421,10 @@
             q_ref[t] = qkv[:, :width]
             kv_ref[steps + t] = qkv[:, width:]
 
-            @pl.when(earlier & (t == 0))
-            def _():
-                def ready(s, _):
-                    kv_copy(s).wait_recv()
-                    return 0
-
-                lax.fori_loop(0, steps, ready, 0)
-
-            @pl.when(lax.rem(t, qs) == qs - 1)
+            @pl.when(jnp.logical_not(earlier) & (lax.rem(t, qs) == qs - 1))
             def _():
                 time_chunk(t - (qs - 1))
 
-        @pl.when(later & (i == steps - LEAD))
-        def _():
-            pl.semaphore_signal(go_sem, inc=1, device_id={"tm": tm + 1}, device_id_type=MESH)
-
         return 0
 
     lax.fori_loop(0, steps + lines, iteration, 0)
@@ -448,6 +432,23 @@
     @pl.when(later)
     def _():
         kv_copy(steps - 1).start()
+
+    @pl.when(earlier)
+    def _():
+        def ready(s, _):
+            kv_copy(s).wait_recv()
+            return 0
+
+        lax.fori_loop(0, steps, ready, 0)
+
+        def chunk(n, _):
+            time_chunk(n * qs)
+            return 0
+
+        lax.fori_loop(0, steps // qs, chunk, 0)
+
+    @pl.when(later)
+    def _():
         edge_copy().wait_recv()
         edge_out[...] = edge_in[...]
 
@@ -525,7 +526,6 @@
             dma((steps,)),
             dma((steps,)),
             dma((2,)),
-            pltpu.SemaphoreType.REGULAR,
         ],
         compiler_params=pltpu.CompilerParams(
             collective_id=0, has_side_effects=True, vmem_limit_bytes=58 * 2**20

time: 301 us -> 191 us (0.63)
  Pallas kernels: 291 us -> 182 us
    pallas_call x1, Pallas kernels: 291 us -> 182 us  [row_gather_call(): pl.pallas_call(functools.partial(row_gather_kernel, head), in_specs=[vmem...]
where the time goes in v4:
time: 191 us
  Pallas kernels  182 us (95%)
  local copies, waits for them, and re-layouts  3.95 us (2%)
  starting transfers between devices  3 us (2%)
    pallas_call x1, Pallas kernels, row_gather_call(): pl.pallas_call(functools.partial(row_gather_kernel, head), in_specs=[vmem...  182 us
  transfers between devices with their start and end apart: 1, of which 1 were waited for; matrix products, arithmetic and copies ran while one was open for 0% of the time, Pallas kernels for 0%

profile of v4, /device:TPU:0, one launch (start us, length us, event | category | flops | bytes accessed | tf_op | source)
XLA Modules:
  0.0 191.0 jit_solution(17305124354056326281)
XLA Ops:
  0.6 0.8 copy.13.mine_ref
  1.4 0.0 copy-start
  1.4 3.0 %collective-permute-start = (s32[16,2]{1,0:T(8,128)S(1)}, s32[16,2]{1,0:T(8,128)S(1)}, u32[]{:S(2)}, u32[]{:S(2)}) collective-permute-start(s32[16,2]{1,0:T(8,128)S(1)} %copy.13.mine_ref), channel_id=1, source_target_pairs={{0,2},{2,0},{4,6},{6,4},{8,10},{10,8},{12,14},{14,12},{1,3},{3,1},... | collective-permute-start | bytes 392 | tf_op jit(solution)/shard_map/ppermute | solution.py:558
  4.4 1.6 collective-permute-done.theirs_ref
  6.0 0.0 copy-start.1
  6.0 0.0 copy-done
  6.0 0.6 copy-done.1
  6.6 181.8 %critic_layer.1 = (f32[16,128]{1,0:T(8,128)}, f32[16,128]{1,0:T(8,128)}) custom-call(bf16[16,128,512]{2,1,0:T(8,128)(2,1)} %x_ref.1, s32[16,2]{1,0:T(8,128)} %copy-done, s32[16,2]{1,0:T(8,128)} %copy-done.1, bf16[512,1536]{1,0:T(8,128)(2,1)} %proj.1, bf16[512,512]{1,0:T(8,128)(2,1)} %merge.1, bf16[512,1536]{1,0:T(8,128)(2,1)} %tproj.1, ...), custom_call_target="tpu_custom_call" | custom-call | tf_op jit(solution)/shard_map/critic_layer/pallas_call | solution.py:507
  188.4 1.3 copy.16
  189.7 1.3 copy.17
Async XLA Ops:
  1.4 4.6 %copy-start = (s32[16,2]{1,0:T(8,128)}, s32[16,2]{1,0:T(8,128)S(1)}, u32[]{:S(2)}) copy-start(s32[16,2]{1,0:T(8,128)S(1)} %copy.13.mine_ref) | copy-start | bytes 388
  1.4 4.6 %collective-permute-start = (s32[16,2]{1,0:T(8,128)S(1)}, s32[16,2]{1,0:T(8,128)S(1)}, u32[]{:S(2)}, u32[]{:S(2)}) collective-permute-start(s32[16,2]{1,0:T(8,128)S(1)} %copy.13.mine_ref), channel_id=1, source_target_pairs={{0,2},{2,0},{4,6},{6,4},{8,10},{10,8},{12,14},{14,12},{1,3},{3,1},... | collective-permute-start | bytes 392 | tf_op jit(solution)/shard_map/ppermute | solution.py:558
  6.0 0.6 copy-start.1
